TPU v7x, 32 devices: a whole 2x2x4 slice. The times are simulated.
32 devices in a mesh: shot: 8 (over z, x), sub: 4 (over y, core).
Axes of the slice: x: 2, y: 2, z: 4, core: 2. Of those that a mesh axis runs over, the one named last changes fastest.
Arguments:
- courant: float32 [8, 128, 128, 128], P('shot', 'sub'), may hold values from 0.04 to 0.2
- adjoint_prev: float32 [8, 128, 128, 128], P('shot', 'sub'), may hold values from -6 to 6
- adjoint_now: float32 [8, 128, 128, 128], P('shot', 'sub'), may hold values from -6 to 6
- forward_accel: float32 [8, 4, 128, 128, 128], P('shot', None, 'sub'), may hold values from -6 to 6
- traces: float32 [8, 4, 512], P('shot'), may hold values from -24 to 24
- receivers: int32 [8, 512], P('shot'), may hold values from 0 to 2097151
- owners: int32 [8, 4, 16, 1], P('shot', 'sub'), may hold values from 0 to 7; in each aligned block of 16 rows (0 to 15, 16 to 31, ..., all dimensions but the last counted through in order) at most 2 rows name the same one
- tile_slot: int32 [8, 4, 16], P('shot', 'sub'), may hold values from 0 to 7
Outputs:
- smoothed: float32 [64, 128, 8, 128], P('shot', 'sub')
- adjoint_last: float32 [8, 128, 128, 128], P('shot', 'sub')
Inputs may be any that keep to these rules, and one draw needn't show every extreme that they name: `owners`: among the 16 blocks of one device at most 2 name the same owner, and in some device's blocks one owner is named by exactly 2.
All inputs are finite; a program needn't handle non-finite values.
Results may differ from a plain program's by a relative error of at most 0.00013.
Values sent between devices are 32-bit elements; how exact they have to be, the bound alone decides.
A program may use at most 128 MiB of HBM per device.

v0:
```python
import jax
import jax.numpy as jnp
from jax import lax
from jax.sharding import PartitionSpec as P

TX = 8
TILES_OWN = 8
CAP = 2
STEPS = 4


stencil_weights = (-205.0 / 72.0, 8.0 / 5.0, -1.0 / 5.0, 8.0 / 315.0, -1.0 / 560.0)


def with_halo(array, sides, width):
    for axis, dim in sides:
        size, length = (lax.axis_size(axis), array.shape[dim])
        up = [(i, (i + 1) % size) for i in range(size - 1)]
        down = [(j, i) for i, j in up]
        last = lax.slice_in_dim(array, length - width, length, axis=dim)
        initial = lax.slice_in_dim(array, 0, width, axis=dim)
        before = lax.ppermute(last, axis, up)
        after = lax.ppermute(initial, axis, down)
        array = jnp.concatenate([before, array, after], axis=dim)
    return array


def laplace_eight(padded, depth_len, rows_x, cols_y):
    centre = padded[4 : 4 + depth_len, 4 : 4 + rows_x, 4 : 4 + cols_y]
    summed = 3.0 * stencil_weights[0] * centre
    for distance in range(1, 5):
        factor = stencil_weights[distance]
        pairs = padded[4 + distance : 4 + distance + depth_len, 4 : 4 + rows_x, 4 : 4 + cols_y]
        pairs = (
            pairs + padded[4 - distance : 4 - distance + depth_len, 4 : 4 + rows_x, 4 : 4 + cols_y]
        )
        pairs = (
            pairs + padded[4 : 4 + depth_len, 4 + distance : 4 + distance + rows_x, 4 : 4 + cols_y]
        )
        pairs = (
            pairs + padded[4 : 4 + depth_len, 4 - distance : 4 - distance + rows_x, 4 : 4 + cols_y]
        )
        pairs = (
            pairs + padded[4 : 4 + depth_len, 4 : 4 + rows_x, 4 + distance : 4 + distance + cols_y]
        )
        pairs = (
            pairs + padded[4 : 4 + depth_len, 4 : 4 + rows_x, 4 - distance : 4 - distance + cols_y]
        )
        summed = summed + factor * pairs
    return summed


def band_matrix(depth_len, band_reach):
    row_ids = jnp.arange(depth_len)[:, None]
    col_ids = jnp.arange(depth_len)[None, :]
    distance = (row_ids - col_ids).astype(jnp.float32)
    weights = jnp.where(
        jnp.abs(row_ids - col_ids) <= band_reach,
        jnp.exp(-((2.0 * distance / band_reach) ** 2)),
        0.0,
    )
    return weights / jnp.sum(weights, axis=1, keepdims=True)


def body(courant, adjoint_prev, adjoint_now, forward_accel, traces, receivers, owners, tile_slot):
    sub_count = lax.axis_size("sub")
    shot_count = lax.axis_size("shot")
    sub_index = lax.axis_index("sub")
    depth_len = courant.shape[1]
    rows_x = courant.shape[2]
    cols_y = courant.shape[3]
    speed = courant[0]
    previous = adjoint_prev[0]
    current = adjoint_now[0]
    slab_cells = depth_len * rows_x * cols_y
    offset = receivers[0] - sub_index * slab_cells
    inside = (offset >= 0) & (offset < slab_cells)
    local_index = jnp.where(inside, offset, 0)
    gradient = jnp.zeros_like(current)
    for time_step in range(STEPS):
        extended = with_halo(current, (("sub", 0),), 4)
        padded = jnp.pad(extended, ((0, 0), (4, 4), (4, 4)))
        advanced = (
            2.0 * current - previous + speed * laplace_eight(padded, depth_len, rows_x, cols_y)
        )
        values = jnp.where(inside, traces[0, time_step], 0.0)
        advanced = advanced.reshape(-1).at[local_index].add(values).reshape(current.shape)
        gradient = gradient + advanced * forward_accel[0, time_step]
        previous, current = (current, advanced)
    block_count = rows_x // TX
    blocks = gradient.reshape(depth_len, block_count, TX * cols_y)
    owners_here = owners[0, 0, :, 0]
    slots_here = tile_slot[0, 0, :]
    same_owner = owners_here[:, None] == owners_here[None, :]
    block_ids = jnp.arange(block_count)
    earlier = block_ids[None, :] < block_ids[:, None]
    earlier_count = jnp.sum(same_owner & earlier, axis=1)
    position = owners_here * CAP + earlier_count
    slot_ids = jnp.arange(shot_count * CAP)
    placed = slot_ids[:, None] == position[None, :]
    send_data = jnp.einsum(
        "sk,zkc->szc", placed.astype(jnp.float32), blocks, precision=lax.Precision.HIGHEST
    )
    send_ids = jnp.sum(jnp.where(placed, slots_here[None, :] + 1, 0), axis=1) - 1
    received, received_ids = (
        lax.all_to_all(send_data, "shot", split_axis=0, concat_axis=0, tiled=True),
        lax.all_to_all(send_ids, "shot", split_axis=0, concat_axis=0, tiled=True),
    )
    picked = (jnp.arange(TILES_OWN)[:, None] == received_ids[None, :]).astype(jnp.float32)
    owned_flat = jnp.einsum("ts,szc->tzc", picked, received, precision=lax.Precision.HIGHEST)
    owned_tiles = owned_flat.reshape(TILES_OWN, depth_len, TX, cols_y)
    full_band = band_matrix(depth_len * sub_count, depth_len)
    pencils = lax.all_to_all(owned_tiles, "sub", split_axis=2, concat_axis=1, tiled=True)
    smoothed_cols = jnp.einsum("ij,tjxy->tixy", full_band, pencils, precision=lax.Precision.HIGHEST)
    smoothed = lax.all_to_all(smoothed_cols, "sub", split_axis=1, concat_axis=2, tiled=True)
    return (smoothed, current[None])


def solution(mesh):
    placed = (
        P("shot", "sub", None, None),
        P("shot", "sub", None, None),
        P("shot", "sub", None, None),
        P("shot", None, "sub", None, None),
        P("shot", None, None),
        P("shot", None),
        P("shot", "sub", None, None),
        P("shot", "sub", None),
    )
    return jax.shard_map(
        body,
        mesh=mesh,
        in_specs=placed,
        out_specs=(P("shot", "sub", None, None), P("shot", "sub", None, None)),
        check_vma=False,
    )
```

profile of v0, /device:TPU:0, one launch (start us, length us, event | category | flops | bytes accessed | tf_op | source)
XLA Modules:
  0.0 390.0 jit_solution(5312718330011647066)
XLA Ops:
  3.0 3.0 collective-permute-start.1
  9.0 6.5 %select_maximum_fusion.6 = f32[40,136,136]{2,1,0:T(8,128)} fusion(f32[4,128,128]{2,1,0:T(8,128)S(1)} %collective-permute-done, f32[32,128,128]{2,1,0:T(8,128)} %bitcast.85, f32[4,128,128]{2,1,0:T(8,128)S(1)} %collective-permute-done.1), kind=kLoop, calls=%fused_computation.14 | loop fusion | flops 11097600 | bytes 5580800 | tf_op jit(solution)/shard_map/concatenate | solution.py:24
  15.5 43.2 %fusion.103 = f32[32,128,128]{2,1,0:T(8,128)S(1)} fusion(f32[32,128,128]{2,1,0:T(8,128)} %bitcast.86, f32[4,128,128]{2,1,0:T(8,128)S(1)} %collective-permute-done.1, f32[4,128,128]{2,1,0:T(8,128)S(1)} %collective-permute-done, f32[40,136,136]{2,1,0:T(8,128)} %select_maximum_fusion.6, f32[1,32,128,128]{3,2,1,0:T(8,128)} %param.8, f32[1,32,128,128]{3,2,1,0:T(8,128)} %param.9), kind=kLoop, calls=%fused_computation.167 | loop fusion | flops 21495808 | bytes 42467328 | tf_op jit(solution)/shard_map/add | solution.py:84
  58.8 4.2 %scatter_fusion = f32[524288]{0:T(1024)S(1)} fusion(f32[524288]{0:T(1024)S(1)} %bitcast.74, s32[512]{0:T(512)S(1)} %bitcast.98, f32[512]{0:T(512)S(1)} %get-tuple-element.27), kind=kCustom, calls=%fused_computation | custom fusion | flops 512 | bytes 8192 | tf_op jit(solution)/shard_map/scatter-add | solution.py:87
  64.3 5.8 %collective-permute-start.3 = (f32[4,128,128]{2,1,0:T(8,128)S(1)}, f32[4,128,128]{2,1,0:T(8,128)S(1)}, u32[]{:S(2)}, u32[]{:S(2)}) collective-permute-start(f32[4,128,128]{2,1,0:T(8,128)S(1)} %bitcast.96), channel_id=1, source_target_pairs={{0,1},{1,2},{2,3},{4,5},{5,6},{6,7},{8,9},{9,10},{10,11},{12,13},{... | collective-permute-start | bytes 786440 | tf_op jit(solution)/shard_map/ppermute | solution.py:22
  70.9 5.3 %select_maximum_fusion.4 = f32[40,136,136]{2,1,0:T(8,128)} fusion(f32[4,128,128]{2,1,0:T(8,128)S(1)} %collective-permute-done.2, f32[32,128,128]{2,1,0:T(8,128)S(1)} %bitcast.75, f32[4,128,128]{2,1,0:T(8,128)S(1)} %collective-permute-done.3), kind=kLoop, calls=%fused_computation.12 | loop fusion | flops 11097600 | bytes 5580800 | tf_op jit(solution)/shard_map/concatenate | solution.py:24
  76.3 39.5 %fusion.73 = f32[32,128,128]{2,1,0:T(8,128)} fusion(f32[32,128,128]{2,1,0:T(8,128)S(1)} %bitcast.76, f32[4,128,128]{2,1,0:T(8,128)S(1)} %collective-permute-done.3, f32[4,128,128]{2,1,0:T(8,128)S(1)} %collective-permute-done.2, f32[40,136,136]{2,1,0:T(8,128)} %select_maximum_fusion.4, f32[1,32,128,128]{3,2,1,0:T(8,128)} %param.8, f32[1,32,128,128]{3,2,1,0:T(8,128)} %param.10), kind=kLoop, calls=%fused_computation.137 | loop fusion | flops 21495808 | bytes 42467328 | tf_op jit(solution)/shard_map/add | solution.py:84
  115.8 6.2 %scatter_fusion.1 = f32[524288]{0:T(1024)} fusion(f32[524288]{0:T(1024)} %bitcast.78, s32[512]{0:T(512)S(1)} %bitcast.99, f32[512]{0:T(512)S(1)} %get-tuple-element.26), kind=kCustom, calls=%fused_computation.1 | custom fusion | flops 512 | bytes 8192 | tf_op jit(solution)/shard_map/scatter-add | solution.py:87
  124.4 7.1 %collective-permute-start.5 = (f32[4,128,128]{2,1,0:T(8,128)S(1)}, f32[4,128,128]{2,1,0:T(8,128)S(1)}, u32[]{:S(2)}, u32[]{:S(2)}) collective-permute-start(f32[4,128,128]{2,1,0:T(8,128)S(1)} %bitcast.94), channel_id=1, source_target_pairs={{0,1},{1,2},{2,3},{4,5},{5,6},{6,7},{8,9},{9,10},{10,11},{12,13},{... | collective-permute-start | bytes 786440 | tf_op jit(solution)/shard_map/ppermute | solution.py:22
  132.3 6.5 %all-to-all-start = ((s32[8,2,1]{1,2,0:T(1,128)}), s32[8,2,1]{1,2,0:T(1,128)S(1)}, u32[]{:S(2)}, u32[]{:S(2)}) async-start(s32[8,2,1]{1,2,0:T(1,128)} %bitcast.2), calls=%async_computation | async-start | bytes 8192 | tf_op jit(solution)/shard_map/all_to_all | solution.py:107
  138.8 6.5 %select_maximum_fusion.2 = f32[40,136,136]{2,1,0:T(8,128)} fusion(f32[4,128,128]{2,1,0:T(8,128)S(1)} %collective-permute-done.4, f32[32,128,128]{2,1,0:T(8,128)} %bitcast.79, f32[4,128,128]{2,1,0:T(8,128)S(1)} %collective-permute-done.5), kind=kLoop, calls=%fused_computation.10 | loop fusion | flops 11097600 | bytes 5580800 | tf_op jit(solution)/shard_map/concatenate | solution.py:24
  145.3 44.4 %fusion.43 = f32[32,128,128]{2,1,0:T(8,128)} fusion(f32[32,128,128]{2,1,0:T(8,128)} %bitcast.80, f32[4,128,128]{2,1,0:T(8,128)S(1)} %collective-permute-done.5, f32[4,128,128]{2,1,0:T(8,128)S(1)} %collective-permute-done.4, f32[40,136,136]{2,1,0:T(8,128)} %select_maximum_fusion.2, f32[1,32,128,128]{3,2,1,0:T(8,128)} %param.8, f32[32,128,128]{2,1,0:T(8,128)S(1)} %bitcast.77), kind=kLoop, calls=%fused_computation.107 | loop fusion | flops 21495808 | bytes 42467328 | tf_op jit(solution)/shard_map/add | solution.py:84
  189.7 6.2 %scatter_fusion.2 = f32[524288]{0:T(1024)} fusion(f32[524288]{0:T(1024)} %bitcast.82, s32[512]{0:T(512)S(1)} %bitcast.100, f32[512]{0:T(512)S(1)} %get-tuple-element.25), kind=kCustom, calls=%fused_computation.2 | custom fusion | flops 512 | bytes 8192 | tf_op jit(solution)/shard_map/scatter-add | solution.py:87
  199.0 4.9 %collective-permute-start.7 = (f32[4,128,128]{2,1,0:T(8,128)S(1)}, f32[4,128,128]{2,1,0:T(8,128)S(1)}, u32[]{:S(2)}, u32[]{:S(2)}) collective-permute-start(f32[4,128,128]{2,1,0:T(8,128)S(1)} %bitcast.93), channel_id=1, source_target_pairs={{0,1},{1,2},{2,3},{4,5},{5,6},{6,7},{8,9},{9,10},{10,11},{12,13},{... | collective-permute-start | bytes 786440 | tf_op jit(solution)/shard_map/ppermute | solution.py:22
  203.8 7.1 %fusion.161 = (f32[1,1,32,128,128]{4,3,2,1,0:T(8,128)}, f32[1,1,32,128,128]{4,3,2,1,0:T(8,128)}, f32[1,1,32,128,128]{4,3,2,1,0:T(8,128)}, f32[1,1,32,128,128]{4,3,2,1,0:T(8,128)}) fusion(f32[1,4,32,128,128]{4,3,2,1,0:T(8,128)} %param.11), kind=kLoop, calls=%fused_computation.266 | loop fusion | bytes 16777216 | tf_op jit(solution)/shard_map/slice | solution.py:88
  210.9 2.7 squeeze.42
  213.6 2.8 squeeze.44
  216.4 2.7 squeeze.46
  219.1 2.8 squeeze.48
  223.4 2.8 reshape.182
  227.7 5.4 %select_maximum_fusion = f32[40,136,136]{2,1,0:T(8,128)} fusion(f32[4,128,128]{2,1,0:T(8,128)S(1)} %collective-permute-done.6, f32[32,128,128]{2,1,0:T(8,128)S(1)} %bitcast.83, f32[4,128,128]{2,1,0:T(8,128)S(1)} %collective-permute-done.7), kind=kLoop, calls=%fused_computation.8 | loop fusion | flops 11097600 | bytes 5580800 | tf_op jit(solution)/shard_map/concatenate | solution.py:24
  233.1 39.5 %fusion.13 = f32[32,128,128]{2,1,0:T(8,128)} fusion(f32[32,128,128]{2,1,0:T(8,128)S(1)} %bitcast.84, f32[4,128,128]{2,1,0:T(8,128)S(1)} %collective-permute-done.7, f32[4,128,128]{2,1,0:T(8,128)S(1)} %collective-permute-done.6, f32[40,136,136]{2,1,0:T(8,128)} %select_maximum_fusion, f32[1,32,128,128]{3,2,1,0:T(8,128)} %param.8, f32[32,128,128]{2,1,0:T(8,128)S(1)} %bitcast.81), kind=kLoop, calls=%fused_computation.77 | loop fusion | flops 21495808 | bytes 42467328 | tf_op jit(solution)/shard_map/add | solution.py:84
  272.6 6.2 %scatter_fusion.3 = f32[524288]{0:T(1024)} fusion(f32[524288]{0:T(1024)} %bitcast.87, s32[512]{0:T(512)S(1)} %bitcast.101, f32[512]{0:T(512)S(1)} %get-tuple-element.24), kind=kCustom, calls=%fused_computation.3 | custom fusion | flops 512 | bytes 8192 | tf_op jit(solution)/shard_map/scatter-add | solution.py:87
  278.8 2.9 reshape.188
  281.7 6.9 %fusion.133 = f32[16,32,1024]{2,0,1:T(8,128)S(1)} fusion(f32[32,16,1024]{2,1,0:T(8,128)} %reshape.188, f32[32,16,1024]{2,1,0:T(8,128)} %squeeze.48, f32[32,16,1024]{2,1,0:T(8,128)} %reshape.185, f32[32,16,1024]{2,1,0:T(8,128)} %squeeze.46, f32[32,16,1024]{2,1,0:T(8,128)} %reshape.182, f32[32,16,1024]{2,1,0:T(8,128)} %squeeze.44, ...), kind=kOutput, calls=%fused_computation.222 | convolution fusion | flops 104333568 | bytes 18874432 | tf_op jit(solution)/shard_map/sk,zkc->szc/dot_general | solution.py:101
  288.6 2.6 copy.32
  291.2 6.0 %all-to-all-start.1 = ((f32[16,32,1024]{2,1,0:T(8,128)}), f32[16,32,1024]{2,1,0:T(8,128)S(1)}, u32[]{:S(2)}, u32[]{:S(2)}) async-start(f32[16,32,1024]{2,1,0:T(8,128)} %copy.32), calls=%async_computation.1 | async-start | bytes 4194304 | tf_op jit(solution)/shard_map/all_to_all | solution.py:106
  298.4 48.2 %all-to-all-done.1 = f32[16,32,1024]{2,1,0:T(8,128)S(1)} async-done(((f32[16,32,1024]{2,1,0:T(8,128)}), f32[16,32,1024]{2,1,0:T(8,128)S(1)}, u32[]{:S(2)}, u32[]{:S(2)}) %all-to-all-start.1) | async-done | bytes 2097184 | tf_op jit(solution)/shard_map/all_to_all | solution.py:106
  346.6 2.0 fusion.141
  350.2 3.5 all-to-all-start.2
  353.8 14.3 %all-to-all-done.2 = f32[8,32,8,128]{3,1,0,2:T(8,128)S(1)} async-done(((f32[8,32,8,128]{3,1,0,2:T(8,128)}), f32[8,32,8,128]{3,1,0,2:T(8,128)S(1)}, u32[]{:S(2)}, u32[]{:S(2)}) %all-to-all-start.2) | async-done | bytes 1048608 | tf_op jit(solution)/shard_map/all_to_all | solution.py:113
  370.9 16.9 %all_to_all.47 = f32[8,128,2,128]{3,2,0,1:T(2,128)S(1)} all-to-all(f32[8,128,2,128]{3,2,0,1:T(2,128)S(1)} %copy.38), channel_id=1, replica_groups=mesh['shot'=8,'sub'=4] {'sub'}, dimensions={1} | all-to-all | bytes 2097152 | tf_op jit(solution)/shard_map/all_to_all | solution.py:115
  (48 shorter events, 24.3 us)
Async XLA Ops:
  1.7 7.3 %collective-permute-start = (f32[4,128,128]{2,1,0:T(8,128)S(1)}, f32[4,128,128]{2,1,0:T(8,128)S(1)}, u32[]{:S(2)}, u32[]{:S(2)}) collective-permute-start(f32[4,128,128]{2,1,0:T(8,128)S(1)} %get-tuple-element.18), channel_id=1, source_target_pairs={{1,0},{2,1},{3,2},{5,4},{6,5},{7,6},{9,8},{10,9},{11,10},{13,12},{... | collective-permute-start | bytes 786440 | tf_op jit(solution)/shard_map/ppermute | solution.py:23
  3.0 6.0 %collective-permute-start.1 = (f32[4,128,128]{2,1,0:T(8,128)S(1)}, f32[4,128,128]{2,1,0:T(8,128)S(1)}, u32[]{:S(2)}, u32[]{:S(2)}) collective-permute-start(f32[4,128,128]{2,1,0:T(8,128)S(1)} %get-tuple-element.19), channel_id=1, source_target_pairs={{0,1},{1,2},{2,3},{4,5},{5,6},{6,7},{8,9},{9,10},{10,11},{12,13},{... | collective-permute-start | bytes 786440 | tf_op jit(solution)/shard_map/ppermute | solution.py:22
  58.7 11.3 %copy-start.3 = (s32[1,1,16,1]{2,3,1,0:T(1,128)S(1)}, s32[1,1,16,1]{2,3,1,0:T(1,128)}, u32[]{:S(2)}) copy-start(s32[1,1,16,1]{2,3,1,0:T(1,128)} %param.14) | copy-start | bytes 196
  63.0 7.3 %collective-permute-start.2 = (f32[4,128,128]{2,1,0:T(8,128)S(1)}, f32[4,128,128]{2,1,0:T(8,128)S(1)}, u32[]{:S(2)}, u32[]{:S(2)}) collective-permute-start(f32[4,128,128]{2,1,0:T(8,128)S(1)} %bitcast.97), channel_id=1, source_target_pairs={{1,0},{2,1},{3,2},{5,4},{6,5},{7,6},{9,8},{10,9},{11,10},{13,12},{... | collective-permute-start | bytes 786440 | tf_op jit(solution)/shard_map/ppermute | solution.py:23
  64.3 6.6 %collective-permute-start.3 = (f32[4,128,128]{2,1,0:T(8,128)S(1)}, f32[4,128,128]{2,1,0:T(8,128)S(1)}, u32[]{:S(2)}, u32[]{:S(2)}) collective-permute-start(f32[4,128,128]{2,1,0:T(8,128)S(1)} %bitcast.96), channel_id=1, source_target_pairs={{0,1},{1,2},{2,3},{4,5},{5,6},{6,7},{8,9},{9,10},{10,11},{12,13},{... | collective-permute-start | bytes 786440 | tf_op jit(solution)/shard_map/ppermute | solution.py:22
  123.1 15.7 %collective-permute-start.4 = (f32[4,128,128]{2,1,0:T(8,128)S(1)}, f32[4,128,128]{2,1,0:T(8,128)S(1)}, u32[]{:S(2)}, u32[]{:S(2)}) collective-permute-start(f32[4,128,128]{2,1,0:T(8,128)S(1)} %bitcast.95), channel_id=1, source_target_pairs={{1,0},{2,1},{3,2},{5,4},{6,5},{7,6},{9,8},{10,9},{11,10},{13,12},{... | collective-permute-start | bytes 786440 | tf_op jit(solution)/shard_map/ppermute | solution.py:23
  124.4 14.4 %collective-permute-start.5 = (f32[4,128,128]{2,1,0:T(8,128)S(1)}, f32[4,128,128]{2,1,0:T(8,128)S(1)}, u32[]{:S(2)}, u32[]{:S(2)}) collective-permute-start(f32[4,128,128]{2,1,0:T(8,128)S(1)} %bitcast.94), channel_id=1, source_target_pairs={{0,1},{1,2},{2,3},{4,5},{5,6},{6,7},{8,9},{9,10},{10,11},{12,13},{... | collective-permute-start | bytes 786440 | tf_op jit(solution)/shard_map/ppermute | solution.py:22
  132.3 158.8 %all-to-all-start = ((s32[8,2,1]{1,2,0:T(1,128)}), s32[8,2,1]{1,2,0:T(1,128)S(1)}, u32[]{:S(2)}, u32[]{:S(2)}) async-start(s32[8,2,1]{1,2,0:T(1,128)} %bitcast.2), calls=%async_computation | async-start | bytes 8192 | tf_op jit(solution)/shard_map/all_to_all | solution.py:107
  197.7 30.0 %collective-permute-start.6 = (f32[4,128,128]{2,1,0:T(8,128)}, f32[4,128,128]{2,1,0:T(8,128)S(1)}, u32[]{:S(2)}, u32[]{:S(2)}) collective-permute-start(f32[4,128,128]{2,1,0:T(8,128)} %bitcast.25), channel_id=1, source_target_pairs={{1,0},{2,1},{3,2},{5,4},{6,5},{7,6},{9,8},{10,9},{11,10},{13,12},{... | collective-permute-start | bytes 786440 | tf_op jit(solution)/shard_map/ppermute | solution.py:23
  199.0 28.8 %collective-permute-start.7 = (f32[4,128,128]{2,1,0:T(8,128)S(1)}, f32[4,128,128]{2,1,0:T(8,128)S(1)}, u32[]{:S(2)}, u32[]{:S(2)}) collective-permute-start(f32[4,128,128]{2,1,0:T(8,128)S(1)} %bitcast.93), channel_id=1, source_target_pairs={{0,1},{1,2},{2,3},{4,5},{5,6},{6,7},{8,9},{9,10},{10,11},{12,13},{... | collective-permute-start | bytes 786440 | tf_op jit(solution)/shard_map/ppermute | solution.py:22
  223.4 2.8 copy-start.1
  227.7 5.4 %copy-start = (f32[524288]{0:T(1024)S(1)}, f32[524288]{0:T(1024)}, u32[]{:S(2)}) copy-start(f32[524288]{0:T(1024)} %scatter_fusion.1) | copy-start | bytes 6291460
  278.8 2.9 copy-start.2
  291.2 55.5 %all-to-all-start.1 = ((f32[16,32,1024]{2,1,0:T(8,128)}), f32[16,32,1024]{2,1,0:T(8,128)S(1)}, u32[]{:S(2)}, u32[]{:S(2)}) async-start(f32[16,32,1024]{2,1,0:T(8,128)} %copy.32), calls=%async_computation.1 | async-start | bytes 4194304 | tf_op jit(solution)/shard_map/all_to_all | solution.py:106
  350.2 17.9 %all-to-all-start.2 = ((f32[8,32,8,128]{3,1,0,2:T(8,128)}), f32[8,32,8,128]{3,1,0,2:T(8,128)S(1)}, u32[]{:S(2)}, u32[]{:S(2)}) async-start(f32[8,32,8,128]{3,1,0,2:T(8,128)} %copy.34), calls=%async_computation.2 | async-start | bytes 2097152 | tf_op jit(solution)/shard_map/all_to_all | solution.py:113
where the time goes:
time: 396 us; the launch traced here: 390 us
  other arithmetic  216 us (55%)
  waiting for transfers between devices  63.1 us (16%)
  starting transfers between devices  41.9 us (11%)
  local copies, waits for them, and re-layouts  39.9 us (10%)
  blocking collectives  16.9 us (4%)
  matrix products  10.7 us (3%)
    add x4, other arithmetic, body(): 2.0 * current - previous  167 us
    all_to_all x1, waiting for transfers between devices, body(): lax.all_to_all(send_data, 'shot', split_axis=0, concat_axis=0, tiled=True)  48.2 us
    concatenate x4, other arithmetic, with_halo(): array = jnp.concatenate([before, array, after], axis=dim)  23.7 us
    scatter-add x4, other arithmetic, body(): advanced.reshape(-1).at[local_index].add(values).reshape(current.shape)  22.8 us
    ppermute x4, starting transfers between devices, with_halo(): before = lax.ppermute(last, axis, up)  20.8 us
    all_to_all x1, blocking collectives, body(): lax.all_to_all(smoothed_cols, 'sub', split_axis=1, concat_axis=2, tiled=T...  16.9 us
    all_to_all x1, waiting for transfers between devices, body(): lax.all_to_all(owned_tiles, 'sub', split_axis=2, concat_axis=1, tiled=True)  14.3 us
    squeeze x4, local copies, waits for them, and re-layouts, body(): gradient = gradient + advanced * forward_accel[0, time_step]  11 us
  transfers between devices with their start and end apart: 11, of which 3 were waited for; matrix products, arithmetic and copies ran while one was open for 39% of the time, Pallas kernels for 0%

commit v1 on v0

v1 whole, which is shorter than its diff:
```python
import functools

import jax
import jax.numpy as jnp
from jax import lax
from jax.experimental import pallas as pl
from jax.experimental.pallas import tpu as pltpu
from jax.sharding import PartitionSpec as P

TX = 8
TILES_OWN = 8
CAP = 2
HALO = 4
PAD = 8
MESH = pl.DeviceIdType.MESH

stencil_weights = (-205.0 / 72.0, 8.0 / 5.0, -1.0 / 5.0, 8.0 / 315.0, -1.0 / 560.0)


def prepare_kernel(slab_cells, cols_y, rec_ref, tr_ref, own_ref, slot_ref, src_ref, inv_ref, ids_ref, count_ref):
    steps = src_ref.shape[0]
    zrows = 256

    def zero(i, _):
        src_ref[:, pl.ds(pl.multiple_of(i * zrows, zrows), zrows), :] = jnp.zeros(
            (steps, zrows, cols_y), jnp.float32
        )
        return 0

    lax.fori_loop(0, src_ref.shape[1] // zrows, zero, 0)
    base = lax.axis_index("sub") * slab_cells
    lane = lax.broadcasted_iota(jnp.int32, (1, cols_y), 1)

    def add(r, _):
        off = rec_ref[0, r] - base

        @pl.when((off >= 0) & (off < slab_cells))
        def _():
            row = lax.div(off, cols_y)
            hit = lane == lax.rem(off, cols_y)
            for t in range(steps):
                src_ref[t, pl.ds(row, 1), :] += jnp.where(hit, tr_ref[0, t, r], 0.0)

        return 0

    lax.fori_loop(0, rec_ref.shape[1], add, 0, unroll=4)

    ids_ref[...] = jnp.full(ids_ref.shape, -1, jnp.int32)
    for i in range(count_ref.shape[0]):
        count_ref[i] = 0
    for i in range(inv_ref.shape[0]):
        inv_ref[i] = 0
    for k in range(slot_ref.shape[2]):
        owner = own_ref[0, 0, k, 0]
        place = owner * CAP + count_ref[owner]
        count_ref[owner] = count_ref[owner] + 1
        inv_ref[place] = k
        ids_ref[pl.ds(place, 1)] = jnp.full((1,) + ids_ref.shape[1:], slot_ref[0, 0, k], jnp.int32)


def wave_kernel(
    n_sub, inv_ref, cour_hbm, prev_hbm, now_hbm, acc_hbm, src_hbm,
    last_hbm, send_hbm,
    buf, cour, acc, src, grad, packed,
    lsem, tsem, hsend, hrecv, psem, osem,
):
    me = lax.axis_index("sub")
    steps, depth, rows, cols = acc.shape
    lo, hi = HALO, HALO + depth
    inner = pl.ds(PAD, rows)

    local = [
        pltpu.make_async_copy(now_hbm.at[0], buf.at[0, lo:hi, inner, :], lsem.at[0]),
        pltpu.make_async_copy(prev_hbm.at[0], buf.at[1, lo:hi, inner, :], lsem.at[1]),
        pltpu.make_async_copy(cour_hbm.at[0], cour, lsem.at[2]),
    ]
    per_step = [
        (
            pltpu.make_async_copy(src_hbm.at[t], src.at[t], tsem.at[t, 0]),
            pltpu.make_async_copy(acc_hbm.at[0, t], acc.at[t], tsem.at[t, 1]),
        )
        for t in range(steps)
    ]
    for c in local:
        c.start()
    for t in range(steps):
        for c in per_step[t]:
            c.start()

    for b in range(2):
        buf[b, :, 0:PAD, :] = jnp.zeros((depth + 2 * HALO, PAD, cols), jnp.float32)
        buf[b, :, PAD + rows :, :] = jnp.zeros((depth + 2 * HALO, PAD, cols), jnp.float32)
        buf[b, 0:lo, inner, :] = jnp.zeros((HALO, rows, cols), jnp.float32)
        buf[b, hi:, inner, :] = jnp.zeros((HALO, rows, cols), jnp.float32)

    has_up, has_down = me > 0, me < n_sub - 1
    barrier = pltpu.get_barrier_semaphore()

    @pl.when(has_up)
    def _():
        pl.semaphore_signal(barrier, inc=1, device_id={"sub": me - 1}, device_id_type=MESH)

    @pl.when(has_down)
    def _():
        pl.semaphore_signal(barrier, inc=1, device_id={"sub": me + 1}, device_id_type=MESH)

    pl.semaphore_wait(barrier, jnp.minimum(me, 1) + jnp.minimum(n_sub - 1 - me, 1))

    def halos(t):
        b = t % 2
        if t == 0:
            first, final = now_hbm.at[0, 0:HALO], now_hbm.at[0, depth - HALO : depth]
        else:
            first = buf.at[b, lo : lo + HALO, inner, :]
            final = buf.at[b, hi - HALO : hi, inner, :]
        up = pltpu.make_async_remote_copy(
            src_ref=first, dst_ref=buf.at[b, hi : hi + HALO, inner, :],
            send_sem=hsend.at[t, 0], recv_sem=hrecv.at[t, 0],
            device_id={"sub": me - 1}, device_id_type=MESH,
        )
        down = pltpu.make_async_remote_copy(
            src_ref=final, dst_ref=buf.at[b, 0:HALO, inner, :],
            send_sem=hsend.at[t, 1], recv_sem=hrecv.at[t, 1],
            device_id={"sub": me + 1}, device_id_type=MESH,
        )
        return up, down

    def start_halos(t):
        up, down = halos(t)

        @pl.when(has_up)
        def _():
            up.start()

        @pl.when(has_down)
        def _():
            down.start()

    def wait_halos(t):
        up, down = halos(t)

        @pl.when(has_up)
        def _():
            up.wait_send()
            down.wait_recv()

        @pl.when(has_down)
        def _():
            down.wait_send()
            up.wait_recv()

    start_halos(0)

    lane = lax.broadcasted_iota(jnp.int32, (TX, cols), 1)
    from_left = [None] + [jnp.where(lane >= d, stencil_weights[d], 0.0) for d in range(1, 5)]
    from_right = [None] + [jnp.where(lane < cols - d, stencil_weights[d], 0.0) for d in range(1, 5)]

    def advance(t, chunks):
        cur, nxt = t % 2, (t + 1) % 2

        def block(xb, _):
            x0 = pl.multiple_of(xb * TX, TX)
            own = pl.ds(x0, TX)
            here = pl.ds(pl.multiple_of(x0 + PAD, TX), TX)
            for za, zb in chunks:
                col = {z: buf[cur, z + HALO, here, :] for z in range(za - 4, zb + 4)}
                for z in range(za, zb):
                    c = col[z]
                    lap = (3.0 * stencil_weights[0]) * c
                    for d in range(1, 5):
                        pair = (col[z + d] + col[z - d]) + (
                            buf[cur, z + HALO, pl.ds(x0 + (PAD + d), TX), :]
                            + buf[cur, z + HALO, pl.ds(x0 + (PAD - d), TX), :]
                        )
                        lap = lap + stencil_weights[d] * pair
                        lap = lap + from_left[d] * pltpu.roll(c, d, 1)
                        lap = lap + from_right[d] * pltpu.roll(c, cols - d, 1)
                    adv = (2.0 * c - buf[nxt, z + HALO, here, :]) + (
                        cour[z, own, :] * lap + src[t, z, own, :]
                    )
                    buf[nxt, z + HALO, here, :] = adv
                    g = adv * acc[t, z, own, :]
                    grad[xb, z] = g if t == 0 else grad[xb, z] + g
            return 0

        lax.fori_loop(0, rows // TX, block, 0)

    for c in local:
        c.wait()
    mid = [(z, min(z + 8, depth - HALO)) for z in range(HALO, depth - HALO, 8)]
    for t in range(steps):
        for c in per_step[t]:
            c.wait()
        advance(t, mid)
        wait_halos(t)
        advance(t, [(0, HALO), (depth - HALO, depth)])
        if t + 1 < steps:
            start_halos(t + 1)

    out = pltpu.make_async_copy(buf.at[steps % 2, lo:hi, inner, :], last_hbm.at[0], osem)
    out.start()
    places = packed.shape[0]

    def pack(p, _):
        packed[p] = grad[inv_ref[p]]
        pltpu.make_async_copy(packed.at[p], send_hbm.at[p], psem.at[p]).start()
        return 0

    lax.fori_loop(0, places, pack, 0)

    def drain(p, _):
        pltpu.make_async_copy(packed.at[p], send_hbm.at[p], psem.at[p]).wait()
        return 0

    lax.fori_loop(0, places, drain, 0)
    out.wait()


def tile_kernel(
    n_shot, n_sub, send_hbm, ids_hbm, out_hbm,
    recv, rids, tiles, smooth,
    lsem, dsend, drecv, isend, irecv, nsend, nrecv, osem,
):
    shot, sub = lax.axis_index("shot"), lax.axis_index("sub")
    depth, cols = recv.shape[1], recv.shape[3]
    has_up, has_down = sub > 0, sub < n_sub - 1
    barrier = pltpu.get_barrier_semaphore()
    for i in range(1, n_shot):
        pl.semaphore_signal(
            barrier, inc=1, device_id={"shot": lax.rem(shot + i, n_shot)}, device_id_type=MESH
        )

    @pl.when(has_up)
    def _():
        pl.semaphore_signal(barrier, inc=1, device_id={"sub": sub - 1}, device_id_type=MESH)

    @pl.when(has_down)
    def _():
        pl.semaphore_signal(barrier, inc=1, device_id={"sub": sub + 1}, device_id_type=MESH)

    near = jnp.minimum(sub, 1) + jnp.minimum(n_sub - 1 - sub, 1)
    pl.semaphore_wait(barrier, n_shot - 1 + near)

    def part(i):
        return pl.ds(pl.multiple_of(i * CAP, CAP), CAP)

    copies = []
    for i in range(1, n_shot):
        peer = lax.rem(shot + i, n_shot)
        for src, dst, ss, rs in ((ids_hbm, rids, isend, irecv), (send_hbm, recv, dsend, drecv)):
            copies.append(
                pltpu.make_async_remote_copy(
                    src_ref=src.at[part(peer)], dst_ref=dst.at[CAP * i : CAP * (i + 1)],
                    send_sem=ss.at[i], recv_sem=rs.at[i],
                    device_id={"shot": peer}, device_id_type=MESH,
                )
            )
    for c in copies:
        c.start()
    mine = [
        pltpu.make_async_copy(send_hbm.at[part(shot)], recv.at[0:CAP], lsem.at[0]),
        pltpu.make_async_copy(ids_hbm.at[part(shot)], rids.at[0:CAP], lsem.at[1]),
    ]
    for c in mine:
        c.start()

    band_i = lax.broadcasted_iota(jnp.int32, (depth, 3 * depth), 0)
    band_j = lax.broadcasted_iota(jnp.int32, (depth, 3 * depth), 1) - depth
    there = band_j + sub * depth
    gap = band_i - band_j
    ratio = 2.0 * gap.astype(jnp.float32) / depth
    valid = (jnp.abs(gap) <= depth) & (there >= 0) & (there < n_sub * depth)
    band = jnp.where(valid, jnp.exp(-(ratio * ratio)), 0.0)
    band = band / jnp.sum(band, axis=1, keepdims=True)

    @pl.when(jnp.logical_not(has_up))
    def _():
        tiles[:, 0] = jnp.zeros((TILES_OWN, depth * TX, cols), jnp.float32)

    @pl.when(jnp.logical_not(has_down))
    def _():
        tiles[:, 2] = jnp.zeros((TILES_OWN, depth * TX, cols), jnp.float32)

    def gather(blocks, fresh):
        def layer(z, _):
            rows = pl.ds(pl.multiple_of(z * TX, TX), TX)
            data = [recv[p, z] for p in blocks]
            for t in range(TILES_OWN):
                total = None if fresh else tiles[t, 1, rows, :]
                for p, v in zip(blocks, data):
                    term = jnp.where(rids[p] == t, v, 0.0)
                    total = term if total is None else total + term
                tiles[t, 1, rows, :] = total
            return 0

        lax.fori_loop(0, depth, layer, 0)

    for c in mine:
        c.wait()
    gather(range(CAP), True)
    for i in range(1, n_shot):
        copies[2 * i - 2].wait()
        copies[2 * i - 1].wait()
        gather(range(CAP * i, CAP * (i + 1)), False)

    def edge(t):
        up = pltpu.make_async_remote_copy(
            src_ref=tiles.at[t, 1], dst_ref=tiles.at[t, 2],
            send_sem=nsend.at[t, 0], recv_sem=nrecv.at[t, 0],
            device_id={"sub": sub - 1}, device_id_type=MESH,
        )
        down = pltpu.make_async_remote_copy(
            src_ref=tiles.at[t, 1], dst_ref=tiles.at[t, 0],
            send_sem=nsend.at[t, 1], recv_sem=nrecv.at[t, 1],
            device_id={"sub": sub + 1}, device_id_type=MESH,
        )
        return up, down

    def start_edge(t, _):
        up, down = edge(t)

        @pl.when(has_up)
        def _():
            up.start()

        @pl.when(has_down)
        def _():
            down.start()

        return 0

    lax.fori_loop(0, TILES_OWN, start_edge, 0)

    def finish(t, _):
        up, down = edge(t)

        @pl.when(has_up)
        def _():
            up.wait_send()
            down.wait_recv()

        @pl.when(has_down)
        def _():
            down.wait_send()
            up.wait_recv()

        for x in range(TX):
            pencil = jnp.concatenate(
                [tiles[t, s, pl.ds(x, depth, stride=TX), :] for s in range(3)], axis=0
            )
            smooth[t, pl.ds(x, depth, stride=TX), :] = jnp.dot(
                band, pencil, precision=lax.Precision.HIGHEST, preferred_element_type=jnp.float32
            )
        pltpu.make_async_copy(smooth.at[t], out_hbm.at[t], osem.at[t]).start()
        return 0

    lax.fori_loop(0, TILES_OWN, finish, 0)

    def drain(t, _):
        pltpu.make_async_copy(smooth.at[t], out_hbm.at[t], osem.at[t]).wait()
        return 0

    lax.fori_loop(0, TILES_OWN, drain, 0)


def body(courant, adjoint_prev, adjoint_now, forward_accel, traces, receivers, owners, tile_slot):
    n_sub = lax.axis_size("sub")
    n_shot = lax.axis_size("shot")
    _, steps, depth, rows, cols = forward_accel.shape
    places = n_shot * CAP
    f32 = jnp.float32
    smem = pl.BlockSpec(memory_space=pltpu.SMEM)
    vmem = pl.BlockSpec(memory_space=pltpu.VMEM)
    hbm = pl.BlockSpec(memory_space=pl.ANY)

    source, inverse, ids = pl.pallas_call(
        functools.partial(prepare_kernel, depth * rows * cols, cols),
        out_shape=(
            jax.ShapeDtypeStruct((steps, depth * rows, cols), f32),
            jax.ShapeDtypeStruct((places,), jnp.int32),
            jax.ShapeDtypeStruct((places, 8, cols), jnp.int32),
        ),
        in_specs=[smem] * 4,
        out_specs=(vmem, smem, vmem),
        scratch_shapes=[pltpu.SMEM((n_shot,), jnp.int32)],
        compiler_params=pltpu.CompilerParams(vmem_limit_bytes=32 * 2**20),
        name="prepare",
    )(receivers, traces, owners, tile_slot)
    source = source.reshape(steps, depth, rows, cols)

    last, send = pl.pallas_call(
        functools.partial(wave_kernel, n_sub),
        out_shape=(
            jax.ShapeDtypeStruct((1, depth, rows, cols), f32),
            jax.ShapeDtypeStruct((places, depth, TX, cols), f32),
        ),
        in_specs=[smem] + [hbm] * 5,
        out_specs=(hbm, hbm),
        scratch_shapes=[
            pltpu.VMEM((2, depth + 2 * HALO, rows + 2 * PAD, cols), f32),
            pltpu.VMEM((depth, rows, cols), f32),
            pltpu.VMEM((steps, depth, rows, cols), f32),
            pltpu.VMEM((steps, depth, rows, cols), f32),
            pltpu.VMEM((rows // TX, depth, TX, cols), f32),
            pltpu.VMEM((places, depth, TX, cols), f32),
            pltpu.SemaphoreType.DMA((3,)),
            pltpu.SemaphoreType.DMA((steps, 2)),
            pltpu.SemaphoreType.DMA((steps, 2)),
            pltpu.SemaphoreType.DMA((steps, 2)),
            pltpu.SemaphoreType.DMA((places,)),
            pltpu.SemaphoreType.DMA,
        ],
        compiler_params=pltpu.CompilerParams(
            collective_id=0, has_side_effects=True, vmem_limit_bytes=48 * 2**20
        ),
        name="wave",
    )(inverse, courant, adjoint_prev, adjoint_now, forward_accel, source)

    smoothed = pl.pallas_call(
        functools.partial(tile_kernel, n_shot, n_sub),
        out_shape=jax.ShapeDtypeStruct((TILES_OWN, depth * TX, cols), f32),
        in_specs=[hbm, hbm],
        out_specs=hbm,
        scratch_shapes=[
            pltpu.VMEM((places, depth, TX, cols), f32),
            pltpu.VMEM((places, 8, cols), jnp.int32),
            pltpu.VMEM((TILES_OWN, 3, depth * TX, cols), f32),
            pltpu.VMEM((TILES_OWN, depth * TX, cols), f32),
            pltpu.SemaphoreType.DMA((2,)),
            pltpu.SemaphoreType.DMA((n_shot,)),
            pltpu.SemaphoreType.DMA((n_shot,)),
            pltpu.SemaphoreType.DMA((n_shot,)),
            pltpu.SemaphoreType.DMA((n_shot,)),
            pltpu.SemaphoreType.DMA((TILES_OWN, 2)),
            pltpu.SemaphoreType.DMA((TILES_OWN, 2)),
            pltpu.SemaphoreType.DMA((TILES_OWN,)),
        ],
        compiler_params=pltpu.CompilerParams(
            collective_id=1, has_side_effects=True, vmem_limit_bytes=32 * 2**20
        ),
        name="tiles",
    )(send, ids)
    return (smoothed.reshape(TILES_OWN, depth, TX, cols), last)


def solution(mesh):
    placed = (
        P("shot", "sub", None, None),
        P("shot", "sub", None, None),
        P("shot", "sub", None, None),
        P("shot", None, "sub", None, None),
        P("shot", None, None),
        P("shot", None),
        P("shot", "sub", None, None),
        P("shot", "sub", None),
    )
    return jax.shard_map(
        body,
        mesh=mesh,
        in_specs=placed,
        out_specs=(P("shot", "sub", None, None), P("shot", "sub", None, None)),
        check_vma=False,
    )
```

time: 396 us -> 124 us (0.31)
  the two profiles are of different devices: /device:TPU:0 before, /device:TPU:27 now
where the time goes in v1:
time: 124 us; the launch traced here: 123 us
  Pallas kernels  114 us (92%)
  local copies, waits for them, and re-layouts  8.28 us (7%)
    pallas_call x1, Pallas kernels, body(): pl.pallas_call(functools.partial(tile_kernel, n_shot, n_sub), out_shape=j...  65 us
    pallas_call x1, Pallas kernels, body(): pl.pallas_call(functools.partial(wave_kernel, n_sub), out_shape=(jax.Shap...  40.6 us
    pallas_call x1, Pallas kernels, body(): pl.pallas_call(functools.partial(prepare_kernel, depth * rows * cols, col...  8.87 us
    unnamed x11, local copies, waits for them, and re-layouts  8.28 us

profile of v1, /device:TPU:27, one launch (start us, length us, event | category | flops | bytes accessed | tf_op | source)
XLA Modules:
  0.0 123.4 jit_solution(11642222348751860326)
XLA Ops:
  0.6 0.7 copy.10.own_ref
  1.4 0.0 copy-start.1
  1.4 0.7 copy-done.1
  2.1 0.0 copy-start.2
  2.1 0.7 copy-done.2
  2.7 0.0 copy-start.3
  2.7 0.7 copy-done.3
  3.4 8.9 %prepare.1 = (f32[4,4096,128]{2,1,0:T(8,128)S(1)}, s32[16]{0:T(128)S(1)}, s32[16,8,128]{2,1,0:T(8,128)S(1)}) custom-call(s32[1,512]{1,0:T(1,128)S(1)} %copy-done.2, f32[1,4,512]{2,1,0:T(4,128)S(1)} %copy-done.1, s32[1,1,16,1]{3,2,1,0:T(8,128)S(1)} %copy.10.own_ref, s32[1,1,16]{2,1,0:T(1,128)S(1)} %copy-done.3), custom_call_target="tpu_custom_call" | custom-call | tf_op jit(solution)/shard_map/prepare/pallas_call | solution.py:376
  12.3 0.0 copy-start
  12.3 3.2 %copy-done = f32[4,4096,128]{2,1,0:T(8,128)} copy-done((f32[4,4096,128]{2,1,0:T(8,128)}, f32[4,4096,128]{2,1,0:T(8,128)S(1)}, u32[]{:S(2)}) %copy-start) | copy-done | bytes 8388632
  15.5 40.6 %wave.1 = (f32[1,32,128,128]{3,2,1,0:T(8,128)S(1)}, f32[16,32,8,128]{3,2,1,0:T(8,128)S(1)}) custom-call(s32[16]{0:T(128)S(1)} %get-tuple-element.7.inv_ref, f32[1,32,128,128]{3,2,1,0:T(8,128)} %cour_hbm.1, f32[1,32,128,128]{3,2,1,0:T(8,128)} %prev_hbm.1, f32[1,32,128,128]{3,2,1,0:T(8,128)} %now_hbm.1, f32[1,4,32,128,128]{4,3,2,1,0:T(8,128)} %acc_hbm.1, ...), custom_call_target="tpu_custom_call" | custom-call | tf_op jit(solution)/shard_map/wave/pallas_call | solution.py:391
  56.1 65.0 %tiles.1 = f32[8,256,128]{2,1,0:T(8,128)S(1)} custom-call(f32[16,32,8,128]{3,2,1,0:T(8,128)S(1)} %get-tuple-element.9.send_hbm, s32[16,8,128]{2,1,0:T(8,128)S(1)} %get-tuple-element.10.ids_hbm), custom_call_target="tpu_custom_call" | custom-call | tf_op jit(solution)/shard_map/tiles/pallas_call | solution.py:419
  121.1 1.0 copy.13
  122.1 1.3 %copy.14 = f32[1,32,128,128]{3,2,1,0:T(8,128)} copy(f32[1,32,128,128]{3,2,1,0:T(8,128)S(1)} %get-tuple-element.15) | data formatting | bytes 4194304
Async XLA Ops:
  1.4 0.7 copy-start.1
  2.1 0.7 copy-start.2
  2.7 0.7 copy-start.3
  12.3 3.2 %copy-start = (f32[4,4096,128]{2,1,0:T(8,128)}, f32[4,4096,128]{2,1,0:T(8,128)S(1)}, u32[]{:S(2)}) copy-start(f32[4,4096,128]{2,1,0:T(8,128)S(1)} %get-tuple-element.8) | copy-start | bytes 25165828

commit v2 on v1

--- a/solution.py
+++ b/solution.py
@@ -17,17 +17,18 @@
 stencil_weights = (-205.0 / 72.0, 8.0 / 5.0, -1.0 / 5.0, 8.0 / 315.0, -1.0 / 560.0)
 
 
-def prepare_kernel(slab_cells, cols_y, rec_ref, tr_ref, own_ref, slot_ref, src_ref, inv_ref, ids_ref, count_ref):
-    steps = src_ref.shape[0]
+def prepare_kernel(slab_cells, cols_y, rec_ref, tr_ref, own_ref, slot_ref, *refs):
+    *src_refs, inv_ref, ids_ref, count_ref = refs
     zrows = 256
 
     def zero(i, _):
-        src_ref[:, pl.ds(pl.multiple_of(i * zrows, zrows), zrows), :] = jnp.zeros(
-            (steps, zrows, cols_y), jnp.float32
-        )
-        return 0
-
-    lax.fori_loop(0, src_ref.shape[1] // zrows, zero, 0)
+        for ref in src_refs:
+            ref[pl.ds(pl.multiple_of(i * zrows, zrows), zrows), :] = jnp.zeros(
+                (zrows, cols_y), jnp.float32
+            )
+        return 0
+
+    lax.fori_loop(0, src_refs[0].shape[0] // zrows, zero, 0)
     base = lax.axis_index("sub") * slab_cells
     lane = lax.broadcasted_iota(jnp.int32, (1, cols_y), 1)
 
@@ -38,8 +39,9 @@
         def _():
             row = lax.div(off, cols_y)
             hit = lane == lax.rem(off, cols_y)
-            for t in range(steps):
-                src_ref[t, pl.ds(row, 1), :] += jnp.where(hit, tr_ref[0, t, r], 0.0)
+            old = [ref[pl.ds(row, 1), :] for ref in src_refs]
+            for t, ref in enumerate(src_refs):
+                ref[pl.ds(row, 1), :] = old[t] + jnp.where(hit, tr_ref[0, t, r], 0.0)
 
         return 0
 
@@ -59,11 +61,11 @@
 
 
 def wave_kernel(
-    n_sub, inv_ref, cour_hbm, prev_hbm, now_hbm, acc_hbm, src_hbm,
-    last_hbm, send_hbm,
-    buf, cour, acc, src, grad, packed,
-    lsem, tsem, hsend, hrecv, psem, osem,
+    n_sub, inv_ref, cour_hbm, prev_hbm, now_hbm, acc_hbm, *refs,
 ):
+    steps = acc_hbm.shape[1]
+    src = refs[:steps]
+    last_hbm, send_hbm, buf, cour, acc, grad, packed, lsem, tsem, hsend, hrecv, psem, osem = refs[steps:]
     me = lax.axis_index("sub")
     steps, depth, rows, cols = acc.shape
     lo, hi = HALO, HALO + depth
@@ -75,10 +77,7 @@
         pltpu.make_async_copy(cour_hbm.at[0], cour, lsem.at[2]),
     ]
     per_step = [
-        (
-            pltpu.make_async_copy(src_hbm.at[t], src.at[t], tsem.at[t, 0]),
-            pltpu.make_async_copy(acc_hbm.at[0, t], acc.at[t], tsem.at[t, 1]),
-        )
+        (pltpu.make_async_copy(acc_hbm.at[0, t], acc.at[t], tsem.at[t]),)
         for t in range(steps)
     ]
     for c in local:
@@ -176,7 +175,7 @@
                         lap = lap + from_left[d] * pltpu.roll(c, d, 1)
                         lap = lap + from_right[d] * pltpu.roll(c, cols - d, 1)
                     adv = (2.0 * c - buf[nxt, z + HALO, here, :]) + (
-                        cour[z, own, :] * lap + src[t, z, own, :]
+                        cour[z, own, :] * lap + src[t][z, own, :]
                     )
                     buf[nxt, z + HALO, here, :] = adv
                     g = adv * acc[t, z, own, :]
@@ -218,7 +217,7 @@
 
 def tile_kernel(
     n_shot, n_sub, send_hbm, ids_hbm, out_hbm,
-    recv, rids, tiles, smooth,
+    recv, rids, near, nids, tiles, smooth,
     lsem, dsend, drecv, isend, irecv, nsend, nrecv, osem,
 ):
     shot, sub = lax.axis_index("shot"), lax.axis_index("sub")
@@ -238,8 +237,8 @@
     def _():
         pl.semaphore_signal(barrier, inc=1, device_id={"sub": sub + 1}, device_id_type=MESH)
 
-    near = jnp.minimum(sub, 1) + jnp.minimum(n_sub - 1 - sub, 1)
-    pl.semaphore_wait(barrier, n_shot - 1 + near)
+    beside = jnp.minimum(sub, 1) + jnp.minimum(n_sub - 1 - sub, 1)
+    pl.semaphore_wait(barrier, n_shot - 1 + beside)
 
     def part(i):
         return pl.ds(pl.multiple_of(i * CAP, CAP), CAP)
@@ -281,69 +280,89 @@
     def _():
         tiles[:, 2] = jnp.zeros((TILES_OWN, depth * TX, cols), jnp.float32)
 
-    def gather(blocks, fresh):
+    def gather(data_ref, id_ref, s, i):
         def layer(z, _):
             rows = pl.ds(pl.multiple_of(z * TX, TX), TX)
-            data = [recv[p, z] for p in blocks]
+            blocks = range(CAP * i, CAP * (i + 1))
+            data = [data_ref[p, z] for p in blocks]
             for t in range(TILES_OWN):
-                total = None if fresh else tiles[t, 1, rows, :]
+                total = tiles[t, s, rows, :] if i else None
                 for p, v in zip(blocks, data):
-                    term = jnp.where(rids[p] == t, v, 0.0)
+                    term = jnp.where(id_ref[p] == t, v, 0.0)
                     total = term if total is None else total + term
-                tiles[t, 1, rows, :] = total
+                tiles[t, s, rows, :] = total
             return 0
 
         lax.fori_loop(0, depth, layer, 0)
 
+    def forwards(i):
+        pair = slice(CAP * i, CAP * (i + 1))
+        sources = (send_hbm.at[part(shot)], ids_hbm.at[part(shot)]) if i == 0 else (recv.at[pair], rids.at[pair])
+        both = []
+        for way, peer in ((0, sub - 1), (1, sub + 1)):
+            both.append([
+                pltpu.make_async_remote_copy(
+                    src_ref=source, dst_ref=target.at[way, pair],
+                    send_sem=nsend.at[i, way, kind], recv_sem=nrecv.at[i, way, kind],
+                    device_id={"sub": peer}, device_id_type=MESH,
+                )
+                for kind, (source, target) in enumerate(zip(sources, (near, nids)))
+            ])
+        return both
+
+    def start_forward(i):
+        up, down = forwards(i)
+
+        @pl.when(has_up)
+        def _():
+            for c in up:
+                c.start()
+
+        @pl.when(has_down)
+        def _():
+            for c in down:
+                c.start()
+
+    def take_forward(i):
+        up, down = forwards(i)
+
+        @pl.when(has_up)
+        def _():
+            for c in down:
+                c.wait_recv()
+            gather(near.at[1], nids.at[1], 0, i)
+
+        @pl.when(has_down)
+        def _():
+            for c in up:
+                c.wait_recv()
+            gather(near.at[0], nids.at[0], 2, i)
+
+    start_forward(0)
     for c in mine:
         c.wait()
-    gather(range(CAP), True)
+    gather(recv, rids, 1, 0)
     for i in range(1, n_shot):
         copies[2 * i - 2].wait()
         copies[2 * i - 1].wait()
-        gather(range(CAP * i, CAP * (i + 1)), False)
-
-    def edge(t):
-        up = pltpu.make_async_remote_copy(
-            src_ref=tiles.at[t, 1], dst_ref=tiles.at[t, 2],
-            send_sem=nsend.at[t, 0], recv_sem=nrecv.at[t, 0],
-            device_id={"sub": sub - 1}, device_id_type=MESH,
-        )
-        down = pltpu.make_async_remote_copy(
-            src_ref=tiles.at[t, 1], dst_ref=tiles.at[t, 0],
-            send_sem=nsend.at[t, 1], recv_sem=nrecv.at[t, 1],
-            device_id={"sub": sub + 1}, device_id_type=MESH,
-        )
-        return up, down
-
-    def start_edge(t, _):
-        up, down = edge(t)
+        start_forward(i)
+        gather(recv, rids, 1, i)
+        take_forward(i - 1)
+    take_forward(n_shot - 1)
+    for i in range(n_shot):
+        up, down = forwards(i)
 
         @pl.when(has_up)
         def _():
-            up.start()
+            for c in up:
+                c.wait_send()
 
         @pl.when(has_down)
         def _():
-            down.start()
-
-        return 0
-
-    lax.fori_loop(0, TILES_OWN, start_edge, 0)
+            for c in down:
+                c.wait_send()
 
     def finish(t, _):
-        up, down = edge(t)
-
-        @pl.when(has_up)
-        def _():
-            up.wait_send()
-            down.wait_recv()
-
-        @pl.when(has_down)
-        def _():
-            down.wait_send()
-            up.wait_recv()
-
         for x in range(TX):
             pencil = jnp.concatenate(
                 [tiles[t, s, pl.ds(x, depth, stride=TX), :] for s in range(3)], axis=0
@@ -373,20 +392,20 @@
     vmem = pl.BlockSpec(memory_space=pltpu.VMEM)
     hbm = pl.BlockSpec(memory_space=pl.ANY)
 
-    source, inverse, ids = pl.pallas_call(
+    *source, inverse, ids = pl.pallas_call(
         functools.partial(prepare_kernel, depth * rows * cols, cols),
         out_shape=(
-            jax.ShapeDtypeStruct((steps, depth * rows, cols), f32),
+            *[jax.ShapeDtypeStruct((depth * rows, cols), f32)] * steps,
             jax.ShapeDtypeStruct((places,), jnp.int32),
             jax.ShapeDtypeStruct((places, 8, cols), jnp.int32),
         ),
         in_specs=[smem] * 4,
-        out_specs=(vmem, smem, vmem),
+        out_specs=(*[vmem] * steps, smem, vmem),
         scratch_shapes=[pltpu.SMEM((n_shot,), jnp.int32)],
-        compiler_params=pltpu.CompilerParams(vmem_limit_bytes=32 * 2**20),
+        compiler_params=pltpu.CompilerParams(vmem_limit_bytes=16 * 2**20),
         name="prepare",
     )(receivers, traces, owners, tile_slot)
-    source = source.reshape(steps, depth, rows, cols)
+    source = [field.reshape(depth, rows, cols) for field in source]
 
     last, send = pl.pallas_call(
         functools.partial(wave_kernel, n_sub),
@@ -394,27 +413,26 @@
             jax.ShapeDtypeStruct((1, depth, rows, cols), f32),
             jax.ShapeDtypeStruct((places, depth, TX, cols), f32),
         ),
-        in_specs=[smem] + [hbm] * 5,
+        in_specs=[smem] + [hbm] * 4 + [vmem] * steps,
         out_specs=(hbm, hbm),
         scratch_shapes=[
             pltpu.VMEM((2, depth + 2 * HALO, rows + 2 * PAD, cols), f32),
             pltpu.VMEM((depth, rows, cols), f32),
             pltpu.VMEM((steps, depth, rows, cols), f32),
-            pltpu.VMEM((steps, depth, rows, cols), f32),
             pltpu.VMEM((rows // TX, depth, TX, cols), f32),
             pltpu.VMEM((places, depth, TX, cols), f32),
             pltpu.SemaphoreType.DMA((3,)),
-            pltpu.SemaphoreType.DMA((steps, 2)),
+            pltpu.SemaphoreType.DMA((steps,)),
             pltpu.SemaphoreType.DMA((steps, 2)),
             pltpu.SemaphoreType.DMA((steps, 2)),
             pltpu.SemaphoreType.DMA((places,)),
             pltpu.SemaphoreType.DMA,
         ],
         compiler_params=pltpu.CompilerParams(
-            collective_id=0, has_side_effects=True, vmem_limit_bytes=48 * 2**20
+            collective_id=0, has_side_effects=True, vmem_limit_bytes=40 * 2**20
         ),
         name="wave",
-    )(inverse, courant, adjoint_prev, adjoint_now, forward_accel, source)
+    )(inverse, courant, adjoint_prev, adjoint_now, forward_accel, *source)
 
     smoothed = pl.pallas_call(
         functools.partial(tile_kernel, n_shot, n_sub),
@@ -424,6 +442,8 @@
         scratch_shapes=[
             pltpu.VMEM((places, depth, TX, cols), f32),
             pltpu.VMEM((places, 8, cols), jnp.int32),
+            pltpu.VMEM((2, places, depth, TX, cols), f32),
+            pltpu.VMEM((2, places, 8, cols), jnp.int32),
             pltpu.VMEM((TILES_OWN, 3, depth * TX, cols), f32),
             pltpu.VMEM((TILES_OWN, depth * TX, cols), f32),
             pltpu.SemaphoreType.DMA((2,)),
@@ -431,8 +451,8 @@
             pltpu.SemaphoreType.DMA((n_shot,)),
             pltpu.SemaphoreType.DMA((n_shot,)),
             pltpu.SemaphoreType.DMA((n_shot,)),
-            pltpu.SemaphoreType.DMA((TILES_OWN, 2)),
-            pltpu.SemaphoreType.DMA((TILES_OWN, 2)),
+            pltpu.SemaphoreType.DMA((n_shot, 2, 2)),
+            pltpu.SemaphoreType.DMA((n_shot, 2, 2)),
             pltpu.SemaphoreType.DMA((TILES_OWN,)),
         ],
         compiler_params=pltpu.CompilerParams(

time: 124 us -> 130 us (1.048)
  local copies, waits for them, and re-layouts: 8.28 us -> 13.8 us
    unnamed x11 -> x21, local copies, waits for them, and re-layouts: 8.28 us -> 13.8 us
    pallas_call x1, Pallas kernels: 65 us -> 68.5 us  [body(): pl.pallas_call(functools.partial(tile_kernel, n_shot, n_sub), out_shape=j...]
    pallas_call x1, Pallas kernels: 40.6 us -> 37.6 us  [body(): pl.pallas_call(functools.partial(wave_kernel, n_sub), out_shape=(jax.Shap...]
where the time goes in v2:
time: 130 us
  Pallas kernels  115 us (88%)
  local copies, waits for them, and re-layouts  13.8 us (11%)
    pallas_call x1, Pallas kernels, body(): pl.pallas_call(functools.partial(tile_kernel, n_shot, n_sub), out_shape=j...  68.5 us
    pallas_call x1, Pallas kernels, body(): pl.pallas_call(functools.partial(wave_kernel, n_sub), out_shape=(jax.Shap...  37.6 us
    unnamed x21, local copies, waits for them, and re-layouts  13.8 us
    pallas_call x1, Pallas kernels, body(): pl.pallas_call(functools.partial(prepare_kernel, depth * rows * cols, col...  9.15 us

profile of v2, /device:TPU:27, one launch (start us, length us, event | category | flops | bytes accessed | tf_op | source)
XLA Modules:
  0.0 129.7 jit_solution(8326703867891070093)
XLA Ops:
  0.6 0.7 copy.10.own_ref
  1.4 0.0 copy-start.6
  1.4 0.7 copy-done.6
  2.1 0.0 copy-start.7
  2.1 0.7 copy-done.7
  2.7 0.0 copy-start.8
  2.7 0.7 copy-done.8
  3.4 9.2 %prepare.1 = (f32[4096,128]{1,0:T(8,128)S(1)}, f32[4096,128]{1,0:T(8,128)S(1)}, f32[4096,128]{1,0:T(8,128)S(1)}, f32[4096,128]{1,0:T(8,128)S(1)}, s32[16]{0:T(128)S(1)}, /*index=5*/s32[16,8,128]{2,1,0:T(8,128)S(1)}) custom-call(s32[1,512]{1,0:T(1,128)S(1)} %copy-done.7, f32[1,4,512]{2,1,0:T(4,128)S(1)} %copy-done.6, s32[1,1,16,1]{3,2,1,0:T(8,128)S(1)} %copy.10.own_ref, ...), custom_call_target="tpu_custom_call" | custom-call | tf_op jit(solution)/shard_map/prepare/pallas_call | solution.py:395
  12.6 0.0 copy-start.3
  12.6 1.3 %copy-done.3 = f32[4096,128]{1,0:T(8,128)} copy-done((f32[4096,128]{1,0:T(8,128)}, f32[4096,128]{1,0:T(8,128)S(1)}, u32[]{:S(2)}) %copy-start.3) | copy-done | bytes 2097176
  13.9 0.0 copy-start.4
  13.9 1.3 %copy-done.4 = f32[4096,128]{1,0:T(8,128)} copy-done((f32[4096,128]{1,0:T(8,128)}, f32[4096,128]{1,0:T(8,128)S(1)}, u32[]{:S(2)}) %copy-start.4) | copy-done | bytes 2097176
  15.2 0.0 copy-start.5
  15.2 1.3 %copy-done.5 = f32[4096,128]{1,0:T(8,128)} copy-done((f32[4096,128]{1,0:T(8,128)}, f32[4096,128]{1,0:T(8,128)S(1)}, u32[]{:S(2)}) %copy-start.5) | copy-done | bytes 2097176
  16.5 0.0 copy-start
  16.5 1.6 %copy-done = f32[1,32,128,128]{3,2,1,0:T(8,128)S(1)} copy-done((f32[1,32,128,128]{3,2,1,0:T(8,128)S(1)}, f32[1,32,128,128]{3,2,1,0:T(8,128)}, u32[]{:S(2)}) %copy-start) | copy-done | bytes 2097176
  18.1 0.0 copy-start.1
  18.1 1.6 %copy-done.1 = f32[1,32,128,128]{3,2,1,0:T(8,128)S(1)} copy-done((f32[1,32,128,128]{3,2,1,0:T(8,128)S(1)}, f32[1,32,128,128]{3,2,1,0:T(8,128)}, u32[]{:S(2)}) %copy-start.1) | copy-done | bytes 2097176
  19.7 0.0 copy-start.2
  19.7 1.6 %copy-done.2 = f32[1,32,128,128]{3,2,1,0:T(8,128)S(1)} copy-done((f32[1,32,128,128]{3,2,1,0:T(8,128)S(1)}, f32[1,32,128,128]{3,2,1,0:T(8,128)}, u32[]{:S(2)}) %copy-start.2) | copy-done | bytes 2097176
  21.3 37.6 %wave.1 = (f32[1,32,128,128]{3,2,1,0:T(8,128)S(1)}, f32[16,32,8,128]{3,2,1,0:T(8,128)S(1)}) custom-call(s32[16]{0:T(128)S(1)} %get-tuple-element.10.inv_ref, f32[1,32,128,128]{3,2,1,0:T(8,128)S(1)} %copy-done, f32[1,32,128,128]{3,2,1,0:T(8,128)S(1)} %copy-done.1, f32[1,32,128,128]{3,2,1,0:T(8,128)S(1)} %copy-done.2, f32[1,4,32,128,128]{4,3,2,1,0:T(8,128)} %acc_hbm.1, ...), custom_call_target="tpu_custom_call" | custom-call | tf_op jit(solution)/shard_map/wave/pallas_call | solution.py:410
  58.9 68.5 %tiles.1 = f32[8,256,128]{2,1,0:T(8,128)S(1)} custom-call(f32[16,32,8,128]{3,2,1,0:T(8,128)S(1)} %get-tuple-element.15.send_hbm, s32[16,8,128]{2,1,0:T(8,128)S(1)} %get-tuple-element.16.ids_hbm), custom_call_target="tpu_custom_call" | custom-call | tf_op jit(solution)/shard_map/tiles/pallas_call | solution.py:437
  127.4 1.0 copy.13
  128.4 1.3 %copy.14 = f32[1,32,128,128]{3,2,1,0:T(8,128)} copy(f32[1,32,128,128]{3,2,1,0:T(8,128)S(1)} %get-tuple-element.21) | data formatting | bytes 4194304
Async XLA Ops:
  1.4 0.7 copy-start.6
  2.1 0.7 copy-start.7
  2.7 0.7 copy-start.8
  12.6 1.3 %copy-start.3 = (f32[4096,128]{1,0:T(8,128)}, f32[4096,128]{1,0:T(8,128)S(1)}, u32[]{:S(2)}) copy-start(f32[4096,128]{1,0:T(8,128)S(1)} %get-tuple-element.12) | copy-start | bytes 6291460
  13.9 1.3 %copy-start.4 = (f32[4096,128]{1,0:T(8,128)}, f32[4096,128]{1,0:T(8,128)S(1)}, u32[]{:S(2)}) copy-start(f32[4096,128]{1,0:T(8,128)S(1)} %get-tuple-element.13) | copy-start | bytes 6291460
  15.2 1.3 %copy-start.5 = (f32[4096,128]{1,0:T(8,128)}, f32[4096,128]{1,0:T(8,128)S(1)}, u32[]{:S(2)}) copy-start(f32[4096,128]{1,0:T(8,128)S(1)} %get-tuple-element.14) | copy-start | bytes 6291460
  16.5 1.6 %copy-start = (f32[1,32,128,128]{3,2,1,0:T(8,128)S(1)}, f32[1,32,128,128]{3,2,1,0:T(8,128)}, u32[]{:S(2)}) copy-start(f32[1,32,128,128]{3,2,1,0:T(8,128)} %cour_hbm.1) | copy-start | bytes 6291460
  18.1 1.6 %copy-start.1 = (f32[1,32,128,128]{3,2,1,0:T(8,128)S(1)}, f32[1,32,128,128]{3,2,1,0:T(8,128)}, u32[]{:S(2)}) copy-start(f32[1,32,128,128]{3,2,1,0:T(8,128)} %prev_hbm.1) | copy-start | bytes 6291460
  19.7 1.6 %copy-start.2 = (f32[1,32,128,128]{3,2,1,0:T(8,128)S(1)}, f32[1,32,128,128]{3,2,1,0:T(8,128)}, u32[]{:S(2)}) copy-start(f32[1,32,128,128]{3,2,1,0:T(8,128)} %now_hbm.1) | copy-start | bytes 6291460

commit v3 on v1

--- a/solution.py
+++ b/solution.py
@@ -61,17 +61,18 @@
 def wave_kernel(
     n_sub, inv_ref, cour_hbm, prev_hbm, now_hbm, acc_hbm, src_hbm,
     last_hbm, send_hbm,
-    buf, cour, acc, src, grad, packed,
+    even, odd, cour, acc, src, grad, packed,
     lsem, tsem, hsend, hrecv, psem, osem,
 ):
+    buf = (even, odd)
     me = lax.axis_index("sub")
     steps, depth, rows, cols = acc.shape
     lo, hi = HALO, HALO + depth
     inner = pl.ds(PAD, rows)
 
     local = [
-        pltpu.make_async_copy(now_hbm.at[0], buf.at[0, lo:hi, inner, :], lsem.at[0]),
-        pltpu.make_async_copy(prev_hbm.at[0], buf.at[1, lo:hi, inner, :], lsem.at[1]),
+        pltpu.make_async_copy(now_hbm.at[0], even.at[lo:hi, inner, :], lsem.at[0]),
+        pltpu.make_async_copy(prev_hbm.at[0], odd.at[lo:hi, inner, :], lsem.at[1]),
         pltpu.make_async_copy(cour_hbm.at[0], cour, lsem.at[2]),
     ]
     per_step = [
@@ -87,11 +88,11 @@
         for c in per_step[t]:
             c.start()
 
-    for b in range(2):
-        buf[b, :, 0:PAD, :] = jnp.zeros((depth + 2 * HALO, PAD, cols), jnp.float32)
-        buf[b, :, PAD + rows :, :] = jnp.zeros((depth + 2 * HALO, PAD, cols), jnp.float32)
-        buf[b, 0:lo, inner, :] = jnp.zeros((HALO, rows, cols), jnp.float32)
-        buf[b, hi:, inner, :] = jnp.zeros((HALO, rows, cols), jnp.float32)
+    for ref in buf:
+        ref[:, 0:PAD, :] = jnp.zeros((depth + 2 * HALO, PAD, cols), jnp.float32)
+        ref[:, PAD + rows :, :] = jnp.zeros((depth + 2 * HALO, PAD, cols), jnp.float32)
+        ref[0:lo, inner, :] = jnp.zeros((HALO, rows, cols), jnp.float32)
+        ref[hi:, inner, :] = jnp.zeros((HALO, rows, cols), jnp.float32)
 
     has_up, has_down = me > 0, me < n_sub - 1
     barrier = pltpu.get_barrier_semaphore()
@@ -111,15 +112,15 @@
         if t == 0:
             first, final = now_hbm.at[0, 0:HALO], now_hbm.at[0, depth - HALO : depth]
         else:
-            first = buf.at[b, lo : lo + HALO, inner, :]
-            final = buf.at[b, hi - HALO : hi, inner, :]
+            first = buf[b].at[lo : lo + HALO, inner, :]
+            final = buf[b].at[hi - HALO : hi, inner, :]
         up = pltpu.make_async_remote_copy(
-            src_ref=first, dst_ref=buf.at[b, hi : hi + HALO, inner, :],
+            src_ref=first, dst_ref=buf[b].at[hi : hi + HALO, inner, :],
             send_sem=hsend.at[t, 0], recv_sem=hrecv.at[t, 0],
             device_id={"sub": me - 1}, device_id_type=MESH,
         )
         down = pltpu.make_async_remote_copy(
-            src_ref=final, dst_ref=buf.at[b, 0:HALO, inner, :],
+            src_ref=final, dst_ref=buf[b].at[0:HALO, inner, :],
             send_sem=hsend.at[t, 1], recv_sem=hrecv.at[t, 1],
             device_id={"sub": me + 1}, device_id_type=MESH,
         )
@@ -156,29 +157,32 @@
     from_right = [None] + [jnp.where(lane < cols - d, stencil_weights[d], 0.0) for d in range(1, 5)]
 
     def advance(t, chunks):
-        cur, nxt = t % 2, (t + 1) % 2
+        cur, nxt = buf[t % 2], buf[(t + 1) % 2]
 
         def block(xb, _):
             x0 = pl.multiple_of(xb * TX, TX)
             own = pl.ds(x0, TX)
             here = pl.ds(pl.multiple_of(x0 + PAD, TX), TX)
             for za, zb in chunks:
-                col = {z: buf[cur, z + HALO, here, :] for z in range(za - 4, zb + 4)}
+                col = {z: cur[z + HALO, here, :] for z in range(za - 4, zb + 4)}
+                done = []
                 for z in range(za, zb):
                     c = col[z]
                     lap = (3.0 * stencil_weights[0]) * c
                     for d in range(1, 5):
                         pair = (col[z + d] + col[z - d]) + (
-                            buf[cur, z + HALO, pl.ds(x0 + (PAD + d), TX), :]
-                            + buf[cur, z + HALO, pl.ds(x0 + (PAD - d), TX), :]
+                            cur[z + HALO, pl.ds(x0 + (PAD + d), TX), :]
+                            + cur[z + HALO, pl.ds(x0 + (PAD - d), TX), :]
                         )
                         lap = lap + stencil_weights[d] * pair
                         lap = lap + from_left[d] * pltpu.roll(c, d, 1)
                         lap = lap + from_right[d] * pltpu.roll(c, cols - d, 1)
-                    adv = (2.0 * c - buf[nxt, z + HALO, here, :]) + (
+                    adv = (2.0 * c - nxt[z + HALO, here, :]) + (
                         cour[z, own, :] * lap + src[t, z, own, :]
                     )
-                    buf[nxt, z + HALO, here, :] = adv
+                    done.append(adv)
+                for z, adv in zip(range(za, zb), done):
+                    nxt[z + HALO, here, :] = adv
                     g = adv * acc[t, z, own, :]
                     grad[xb, z] = g if t == 0 else grad[xb, z] + g
             return 0
@@ -197,7 +201,7 @@
         if t + 1 < steps:
             start_halos(t + 1)
 
-    out = pltpu.make_async_copy(buf.at[steps % 2, lo:hi, inner, :], last_hbm.at[0], osem)
+    out = pltpu.make_async_copy(buf[steps % 2].at[lo:hi, inner, :], last_hbm.at[0], osem)
     out.start()
     places = packed.shape[0]
 
@@ -397,7 +401,8 @@
         in_specs=[smem] + [hbm] * 5,
         out_specs=(hbm, hbm),
         scratch_shapes=[
-            pltpu.VMEM((2, depth + 2 * HALO, rows + 2 * PAD, cols), f32),
+            pltpu.VMEM((depth + 2 * HALO, rows + 2 * PAD, cols), f32),
+            pltpu.VMEM((depth + 2 * HALO, rows + 2 * PAD, cols), f32),
             pltpu.VMEM((depth, rows, cols), f32),
             pltpu.VMEM((steps, depth, rows, cols), f32),
             pltpu.VMEM((steps, depth, rows, cols), f32),

time: 124 us -> 124 us (level)
  no operation moved by 1% of the time
where the time goes in v3:
time: 124 us; the launch traced here: 123 us
  Pallas kernels  114 us (92%)
  local copies, waits for them, and re-layouts  8.28 us (7%)
    pallas_call x1, Pallas kernels, body(): pl.pallas_call(functools.partial(tile_kernel, n_shot, n_sub), out_shape=j...  65 us
    pallas_call x1, Pallas kernels, body(): pl.pallas_call(functools.partial(wave_kernel, n_sub), out_shape=(jax.Shap...  40.6 us
    pallas_call x1, Pallas kernels, body(): pl.pallas_call(functools.partial(prepare_kernel, depth * rows * cols, col...  8.83 us
    unnamed x11, local copies, waits for them, and re-layouts  8.28 us

profile of v3, /device:TPU:27, one launch (start us, length us, event | category | flops | bytes accessed | tf_op | source)
XLA Modules:
  0.0 123.4 jit_solution(5953758688294729550)
XLA Ops:
  0.6 0.7 copy.10.own_ref
  1.4 0.0 copy-start.1
  1.4 0.7 copy-done.1
  2.1 0.0 copy-start.2
  2.1 0.7 copy-done.2
  2.7 0.0 copy-start.3
  2.7 0.7 copy-done.3
  3.4 8.8 %prepare.1 = (f32[4,4096,128]{2,1,0:T(8,128)S(1)}, s32[16]{0:T(128)S(1)}, s32[16,8,128]{2,1,0:T(8,128)S(1)}) custom-call(s32[1,512]{1,0:T(1,128)S(1)} %copy-done.2, f32[1,4,512]{2,1,0:T(4,128)S(1)} %copy-done.1, s32[1,1,16,1]{3,2,1,0:T(8,128)S(1)} %copy.10.own_ref, s32[1,1,16]{2,1,0:T(1,128)S(1)} %copy-done.3), custom_call_target="tpu_custom_call" | custom-call | tf_op jit(solution)/shard_map/prepare/pallas_call | solution.py:380
  12.2 0.0 copy-start
  12.2 3.2 %copy-done = f32[4,4096,128]{2,1,0:T(8,128)} copy-done((f32[4,4096,128]{2,1,0:T(8,128)}, f32[4,4096,128]{2,1,0:T(8,128)S(1)}, u32[]{:S(2)}) %copy-start) | copy-done | bytes 8388632
  15.5 40.6 %wave.1 = (f32[1,32,128,128]{3,2,1,0:T(8,128)S(1)}, f32[16,32,8,128]{3,2,1,0:T(8,128)S(1)}) custom-call(s32[16]{0:T(128)S(1)} %get-tuple-element.7.inv_ref, f32[1,32,128,128]{3,2,1,0:T(8,128)} %cour_hbm.1, f32[1,32,128,128]{3,2,1,0:T(8,128)} %prev_hbm.1, f32[1,32,128,128]{3,2,1,0:T(8,128)} %now_hbm.1, f32[1,4,32,128,128]{4,3,2,1,0:T(8,128)} %acc_hbm.1, ...), custom_call_target="tpu_custom_call" | custom-call | tf_op jit(solution)/shard_map/wave/pallas_call | solution.py:395
  56.1 65.0 %tiles.1 = f32[8,256,128]{2,1,0:T(8,128)S(1)} custom-call(f32[16,32,8,128]{3,2,1,0:T(8,128)S(1)} %get-tuple-element.9.send_hbm, s32[16,8,128]{2,1,0:T(8,128)S(1)} %get-tuple-element.10.ids_hbm), custom_call_target="tpu_custom_call" | custom-call | tf_op jit(solution)/shard_map/tiles/pallas_call | solution.py:424
  121.1 1.0 copy.13
  122.0 1.3 %copy.14 = f32[1,32,128,128]{3,2,1,0:T(8,128)} copy(f32[1,32,128,128]{3,2,1,0:T(8,128)S(1)} %get-tuple-element.15) | data formatting | bytes 4194304
Async XLA Ops:
  1.4 0.7 copy-start.1
  2.1 0.7 copy-start.2
  2.7 0.7 copy-start.3
  12.2 3.2 %copy-start = (f32[4,4096,128]{2,1,0:T(8,128)}, f32[4,4096,128]{2,1,0:T(8,128)S(1)}, u32[]{:S(2)}) copy-start(f32[4,4096,128]{2,1,0:T(8,128)S(1)} %get-tuple-element.8) | copy-start | bytes 25165828
